TPU v7x, 32 devices: a whole 2x2x4 slice. The times are simulated.
32 devices in a mesh: groups: 2 (over y), rows: 16 (over z, x, core).
Axes of the slice: x: 2, y: 2, z: 4, core: 2. Of those that a mesh axis runs over, the one named last changes fastest.
Arguments:
- factor_panel: bfloat16 [32768, 2048], P(('groups', 'rows')), parts along dimension 0, may hold values from -0.0625 to 0.0625
- later_adjoint: bfloat16 [32768, 1024], P(('groups', 'rows')), parts along dimension 0, may hold values from -6 to 6
- saved_solution: bfloat16 [32768, 1024], P(('groups', 'rows')), parts along dimension 0, may hold values from -6 to 6
- cotangent: float32 [4096, 1024], P(('groups', 'rows')), parts along dimension 0, may hold values from -6 to 6
- inverse_block: bfloat16 [4096, 2048], P(('groups', 'rows')), parts along dimension 0, as said below
Outputs:
- panel_adjoint: bfloat16 [4096, 1024], P(('groups', 'rows')), parts along dimension 0
- factor_grad: bfloat16 [32768, 2048], P(('groups', 'rows')), parts along dimension 0
There are 2 independent parts, one for each index of `groups`. A program takes and returns all parts, laid end to end along the dimension named above; each array names one. Nothing has to cross between parts.
Inputs may be any that keep to these rules, and one draw needn't show every extreme that they name: inverse_block is zero below its diagonal.
All inputs are finite; a program needn't handle non-finite values.
Results may differ from a plain program's by a relative error of at most 0.0057.
Values may be sent and summed in bfloat16 or wider, within the bound.
No kernel may reach another device: no remote copies, remote signals or barrier semaphores. Data moves between devices by JAX's collectives and lax.ppermute only.
A program may use at most 64 MiB of HBM per device.

v0:
```python
import functools

import jax
import jax.numpy as jnp
from jax import lax
from jax.experimental import pallas as pl
from jax.experimental.pallas import tpu as pltpu
from jax.sharding import PartitionSpec as P


BF, F32 = jnp.bfloat16, jnp.float32
SIZES = (64, 64)
STARTS = tuple(sum(SIZES[:k]) for k in range(len(SIZES)))
CHUNKS = len(SIZES)
VMEM = 24 << 20
FIRST_VMEM = 20 << 20
OUTER_VMEM = 16 << 20


def dot(a, b, ca, cb):
    return lax.dot_general(a, b, (((ca,), (cb,)), ((), ())), preferred_element_type=F32)


def cost(flops, moved):
    return pl.CostEstimate(flops=flops, bytes_accessed=moved, transcendentals=0)


def call(kernel, out_shape, grid, in_specs, out_specs, scratch, flops, moved, limit=VMEM):
    return pl.pallas_call(
        kernel,
        out_shape=out_shape,
        grid_spec=pltpu.PrefetchScalarGridSpec(
            num_scalar_prefetch=1,
            grid=grid,
            in_specs=in_specs,
            out_specs=out_specs,
            scratch_shapes=scratch,
        ),
        compiler_params=pltpu.CompilerParams(vmem_limit_bytes=limit),
        cost_estimate=cost(flops, moved),
    )


WHOLE = pl.BlockSpec(memory_space=pltpu.VMEM)
SCALARS = pl.BlockSpec(memory_space=pltpu.SMEM)


def once(kernel, out_shape, n_in, scratch, flops, moved, limit=VMEM, aliases={}):
    many = isinstance(out_shape, tuple)
    return pl.pallas_call(
        kernel,
        out_shape=out_shape,
        in_specs=[SCALARS] + [WHOLE] * n_in,
        out_specs=(WHOLE,) * len(out_shape) if many else WHOLE,
        scratch_shapes=scratch,
        input_output_aliases=aliases,
        compiler_params=pltpu.CompilerParams(vmem_limit_bytes=limit),
        cost_estimate=cost(flops, moved),
    )


TILE = 512


def first_kernel(groups, ids, l, f, c, *refs):
    n = 2 * len(groups)
    outs, (lv, fv, cv, lt, sems) = refs[:n * CHUNKS], refs[n * CHUNKS:]
    w = l.shape[1] // 8
    own = c.shape[0]
    tiles = f.shape[1] // TILE
    lefts, cots, rights = [], [], []
    for j in range(n):
        at = pl.ds(pl.multiple_of((ids[0] ^ (groups[j // 2] + j % 2)) * w, 128), w)
        lefts.append(pltpu.make_async_copy(l.at[:, at], lv.at[j], sems.at[j]))
        cots.append(pltpu.make_async_copy(c.at[:, at], cv.at[j], sems.at[n + j]))
    for t in range(tiles):
        rights.append(pltpu.make_async_copy(f.at[:, t * TILE:(t + 1) * TILE], fv.at[t], sems.at[2 * n + t]))
    for copy in lefts + rights + cots:
        copy.start()
    for j in range(n):
        lefts[j].wait()
        lt[j * w:(j + 1) * w, :] = lv[j].T
    for t in range(tiles):
        rights[t].wait()
        acc = -dot(lt[...], fv[t], 1, 0)
        if t == 0:
            for copy in cots:
                copy.wait()
        for j in range(n):
            for k in range(CHUNKS):
                out = outs[(j // 2 * CHUNKS + k) * 2 + j % 2]
                at = j * w + STARTS[k]
                out[:, t * TILE:(t + 1) * TILE] = acc[at:at + SIZES[k]].astype(out.dtype)
        for u in range(TILE // own):
            @pl.when(ids[2] == t * (TILE // own) + u)
            def _():
                for j in range(n):
                    both = acc[j * w:(j + 1) * w, u * own:(u + 1) * own] + cv[j].T
                    for k in range(CHUNKS):
                        out = outs[(j // 2 * CHUNKS + k) * 2 + j % 2]
                        got = both[STARTS[k]:STARTS[k] + SIZES[k]]
                        out[:, t * TILE + u * own:t * TILE + (u + 1) * own] = got.astype(out.dtype)


def first(ids, later, panel, cot, groups):
    rows, width = panel.shape
    sides = later.shape[1]
    w = sides // 8
    own = cot.shape[0]
    n = 2 * len(groups)
    shapes = ()
    for _ in groups:
        for s in SIZES:
            shapes += (jax.ShapeDtypeStruct((s, width), F32), jax.ShapeDtypeStruct((s, width), BF))
    return pl.pallas_call(
        functools.partial(first_kernel, groups),
        out_shape=shapes,
        in_specs=[SCALARS] + [pl.BlockSpec(memory_space=pltpu.HBM)] * 3,
        out_specs=(WHOLE,) * len(shapes),
        scratch_shapes=[
            pltpu.VMEM((n, rows, w), BF),
            pltpu.VMEM((width // TILE, rows, TILE), BF),
            pltpu.VMEM((n, own, w), F32),
            pltpu.VMEM((n * w, rows), BF),
            pltpu.SemaphoreType.DMA((2 * n + width // TILE,)),
        ],
        compiler_params=pltpu.CompilerParams(vmem_limit_bytes=FIRST_VMEM),
        cost_estimate=cost(2 * n * w * rows * width, 4 * rows * width),
        name="first",
    )(ids, *(pltpu.with_memory_space_constraint(a, pltpu.HBM) for a in (later, panel, cot)))


def again_kernel(groups, ids, l, f, c, *refs):
    n = len(groups)
    outs, lt = refs[:2 * n * CHUNKS], refs[2 * n * CHUNKS]
    w = l.shape[1] // 8
    own = c.shape[0]
    width = f.shape[1]
    for j in range(2 * n):
        q = groups[j // 2] + j % 2
        at = pl.ds(pl.multiple_of((ids[0] ^ q) * w, 128), w)
        lt[j * w:(j + 1) * w, :] = l[:, at].T
    tile = 512
    for t in range(0, width, tile):
        acc = -dot(lt[...], f[:, t:t + tile], 1, 0)
        for g in range(n):
            for k in range(CHUNKS):
                for s in range(2):
                    out = outs[(g * CHUNKS + k) * 2 + s]
                    at = (2 * g + s) * w + STARTS[k]
                    out[:, t:t + tile] = acc[at:at + SIZES[k]].astype(out.dtype)
        for u in range(tile // own):
            @pl.when(ids[2] == t // own + u)
            def _():
                for j in range(2 * n):
                    q = groups[j // 2] + j % 2
                    rows = c[:, pl.ds(pl.multiple_of((ids[0] ^ q) * w, 128), w)].T
                    both = acc[j * w:(j + 1) * w, u * own:(u + 1) * own] + rows
                    for k in range(CHUNKS):
                        out = outs[(j // 2 * CHUNKS + k) * 2 + j % 2]
                        got = both[STARTS[k]:STARTS[k] + SIZES[k]]
                        out[:, t + u * own:t + (u + 1) * own] = got.astype(out.dtype)


def again(ids, later, panel, cot, groups):
    rows, width = panel.shape
    sides = later.shape[1]
    n = len(groups)
    shapes = ()
    for _ in groups:
        for s in SIZES:
            shapes += (jax.ShapeDtypeStruct((s, width), F32), jax.ShapeDtypeStruct((s, width), BF))
    return once(
        functools.partial(again_kernel, groups),
        shapes,
        3,
        [pltpu.VMEM((n * sides // 4, rows), BF)],
        rows * sides * width * n // 2,
        5 * rows * width,
        FIRST_VMEM,
    )(ids, later, panel, cot)


def order_kernel(ids, s, out):
    w = s.shape[1] // 8
    at = 0
    for k, q in ORDER:
        block = s[:, pl.ds(pl.multiple_of((ids[0] ^ q) * w, 128), w)]
        out[:, at:at + SIZES[k]] = block[:, STARTS[k]:STARTS[k] + SIZES[k]]
        at += SIZES[k]


def order(ids, saved):
    rows, sides = saved.shape
    tile = 256
    return call(
        order_kernel,
        jax.ShapeDtypeStruct((rows, sides), BF),
        (rows // tile,),
        [pl.BlockSpec((tile, sides), lambda t, i: (t, 0))],
        pl.BlockSpec((tile, sides), lambda t, i: (t, 0)),
        [],
        0,
        4 * rows * sides,
    )(ids, saved)


def gather_kernel(places, ids, *refs):
    out = refs[-1]
    for (q, at, size), ref in zip(places, refs):
        own = 128
        out[pl.ds(pl.multiple_of((ids[0] ^ q) * own + at, 16), size), :] = ref[...]


def gather(ids, parts):
    places = tuple((q, at, a.shape[0]) for q, at, a in parts)
    width = parts[0][2].shape[1]
    return call(
        functools.partial(gather_kernel, places),
        jax.ShapeDtypeStruct((8 * 128, width), BF),
        (1,),
        [pl.BlockSpec(a.shape, lambda t, i: (0, 0)) for _, _, a in parts],
        pl.BlockSpec((8 * 128, width), lambda t, i: (0, 0)),
        [],
        0,
        32 * 128 * width,
    )(ids, *[a for _, _, a in parts])


def middle_kernel(ids, r, inv, out):
    out[...] = dot(r[...], inv[...], 1, 1).astype(BF)


def middle(ids, r, inv):
    m, width = r.shape
    n = inv.shape[0]
    return call(
        middle_kernel,
        jax.ShapeDtypeStruct((m, n), BF),
        (1,),
        [pl.BlockSpec((m, width), lambda t, i: (0, 0)), pl.BlockSpec((n, width), lambda t, i: (0, 0))],
        pl.BlockSpec((m, n), lambda t, i: (0, 0)),
        [],
        2 * m * width * n,
        2 * n * width,
    )(ids, r, inv)


def outer_kernel(n_in, lo, first, ids, s, *refs):
    pieces, refs = refs[:n_in], refs[n_in:]
    out = refs[-1]
    depth = sum(p.shape[0] for p in pieces)
    half = out.shape[1] // 2
    for h in range(2):
        for t in range(0, half, 512):
            rhs = jnp.concatenate([p[:, h * half + t:h * half + t + 512] for p in pieces], axis=0)
            got = dot(s[:, lo:lo + depth], rhs, 1, 0)
            at = pl.ds(pl.multiple_of((ids[1] ^ h) * half + t, 512), 512)
            if first:
                out[:, at] = got
            else:
                out[:, at] = refs[0][:, at] + got


def outer(ids, saved, pieces, lo, acc=None):
    rows = saved.shape[0]
    width = pieces[0].shape[1]
    part = sum(p.shape[0] for p in pieces)
    return once(
        functools.partial(outer_kernel, len(pieces), lo, acc is None),
        jax.ShapeDtypeStruct((rows, width), F32),
        1 + len(pieces) + (acc is not None),
        [],
        2 * rows * part * width,
        4 * rows * width,
        OUTER_VMEM,
        {} if acc is None else {2 + len(pieces): 0},
    )(ids, saved, *pieces, *(() if acc is None else (acc,)))


def last_kernel(n_in, lo, ids, s, acc, *refs):
    blocks, (out, adj, held, sems) = refs[:-4], refs[-4:]
    pieces = [blocks[k * 8 + q] for k, q in ORDER[-n_in:]]
    depth = sum(p.shape[0] for p in pieces)
    half = acc.shape[1] // 2
    tiles, tile = held.shape[0], held.shape[2]
    w = adj.shape[1] // 8
    own = adj.shape[0]
    copies = []
    for t in range(tiles):
        h, inner = divmod(t * tile, half)
        at = pl.ds(pl.multiple_of((ids[1] ^ h) * half + inner, tile), tile)
        rhs = jnp.concatenate([p[:, t * tile:(t + 1) * tile] for p in pieces], axis=0)
        held[t] = (-(acc[:, at] + dot(s[:, lo:lo + depth], rhs, 1, 0))).astype(BF)
        copies.append(pltpu.make_async_copy(held.at[t], out.at[:, at], sems.at[t]))
        copies[-1].start()
    mine = pl.ds(pl.multiple_of(ids[0] * own, 128), own)
    for q in range(8):
        block = jnp.concatenate([blocks[k * 8 + q][:, mine] for k in range(CHUNKS)], axis=0)
        adj[:, pl.ds(pl.multiple_of((ids[0] ^ q) * w, 128), w)] = block.T
    for copy in copies:
        copy.wait()


def last(ids, saved, acc, pieces, n_in, lo, own):
    rows, width = acc.shape
    sides = sum(SIZES) * 8
    tiles = 4
    return pl.pallas_call(
        functools.partial(last_kernel, n_in, lo),
        out_shape=(jax.ShapeDtypeStruct((rows, width), BF), jax.ShapeDtypeStruct((own, sides), BF)),
        in_specs=[SCALARS] + [WHOLE] * (2 + len(pieces)),
        out_specs=(pl.BlockSpec(memory_space=pltpu.HBM), WHOLE),
        scratch_shapes=[pltpu.VMEM((tiles, rows, width // tiles), BF), pltpu.SemaphoreType.DMA((tiles,))],
        compiler_params=pltpu.CompilerParams(vmem_limit_bytes=OUTER_VMEM),
        cost_estimate=cost(2 * rows * n_in * pieces[-1].shape[0] * width, 4 * rows * width),
        name="last",
    )(ids, saved, acc, *pieces)


ORDER = (
    (0, 0), (0, 1), (1, 0), (1, 1), (0, 2), (0, 3), (0, 4), (0, 5),
    (1, 2), (1, 3), (1, 4), (1, 5), (0, 6), (0, 7), (1, 6), (1, 7),
)
TAKES = (4, 4, 4, 4)


def make_tiled(n):
    def swap(a, bit):
        return lax.ppermute(a, "rows", [(i, i ^ bit) for i in range(n)])

    def body(factor_panel, later_adjoint, saved_solution, cotangent, inverse_block):
        me = lax.axis_index("rows").astype(jnp.int32)
        own = cotangent.shape[0]
        ids = jnp.stack([me % 8, me // 8, me])

        half = own // 2
        again_inverse = lax.optimization_barrier(inverse_block)
        i2a = swap(inverse_block[:half], 2)
        i4 = swap(inverse_block, 4)
        i2b = swap(again_inverse[half:], 2)
        i6z = swap(i2a, 4)
        i6x = swap(i4[half:], 2)
        firsts = first(ids, later_adjoint, factor_panel, cotangent, (6, 4))
        firsts += again(ids, later_adjoint, factor_panel, cotangent, (2, 0))
        shards = []
        for q, at, a in ((0, 0, inverse_block), (4, 0, i4), (2, 0, i2a), (2, half, i2b), (6, 0, i6z), (6, half, i6x)):
            shards += [(q, at, a), (q + 1, at, swap(a, 1))]
        saved = order(ids, saved_solution)
        inv = gather(ids, shards)

        pieces = []
        acc = None
        for k in range(CHUNKS):
            kept = {}
            for j, g in enumerate((6, 4, 2, 0)):
                keep, send = firsts[(j * CHUNKS + k) * 2:(j * CHUNKS + k) * 2 + 2]
                kept[g] = keep + swap(send, 1).astype(F32)
            u4 = kept[4] + swap(kept[6].astype(BF), 2).astype(F32)
            u0 = kept[0] + swap(kept[2].astype(BF), 2).astype(F32)
            r = u0 + swap(u4.astype(BF), 4).astype(F32)
            r = (r + swap(r.astype(BF), 8).astype(F32)).astype(BF)
            pt = middle(ids, r, inv)
            p = {0: jnp.concatenate([pt, swap(pt, 8)], axis=1)}
            p[2] = swap(p[0], 2)
            p[4] = swap(p[0], 4)
            p[6] = swap(p[4], 2) if k < CHUNKS - 1 else swap(p[2], 4)
            for g in (0, 2, 4, 6):
                p[g + 1] = swap(p[g], 1)
            pieces.append([p[q] for q in range(8)])
        at = lo = 0
        for take in TAKES[:-1]:
            using = [pieces[c][q] for c, q in ORDER[at:at + take]]
            acc = outer(ids, saved, using, lo, acc)
            at += take
            lo += sum(p.shape[0] for p in using)
        grad, adj = last(ids, saved, acc, sum(pieces, []), TAKES[-1], lo, own)
        return adj, grad

    return body


def make_body(n):
    def swap(a, bit):
        return lax.ppermute(a, "rows", [(i, i ^ bit) for i in range(n)])

    rest = [8 << k for k in range(16) if 8 << k < n]

    def body(factor_panel, later_adjoint, saved_solution, cotangent, inverse_block):
        me = lax.axis_index("rows")
        low = me % 8
        sides, panel, own = later_adjoint.shape[1], factor_panel.shape[1], cotangent.shape[0]
        w = sides // 8

        def cols(a, q):
            return lax.dynamic_slice(a, (0, (low ^ q) * w), (a.shape[0], w))

        inv4 = swap(inverse_block, 4)
        kept = {}
        for g in (6, 2, 4, 0):
            pair = jnp.concatenate([cols(later_adjoint, g), cols(later_adjoint, g ^ 1)], axis=1)
            prod = dot(pair, factor_panel, 0, 0)
            cot = jnp.concatenate([cols(cotangent, g), cols(cotangent, g ^ 1)], axis=1).T
            base = lax.dynamic_update_slice(jnp.zeros((2 * w, panel), F32), cot, (0, me * own))
            both = base - prod
            got = swap(both[w:].astype(BF), 1)
            kept[g] = both[:w] + got.astype(F32)
        u4 = kept[4] + swap(kept[6].astype(BF), 2).astype(F32)
        u0 = kept[0] + swap(kept[2].astype(BF), 2).astype(F32)
        r = u0 + swap(u4.astype(BF), 4).astype(F32)
        shards = {0: inverse_block, 4: inv4, 2: swap(inverse_block, 2), 6: swap(inv4, 2)}
        inv = jnp.zeros((8 * own, panel), BF)
        for q in (0, 4, 2, 6):
            inv = lax.dynamic_update_slice(inv, shards[q], ((low ^ q) * own, 0))
            inv = lax.dynamic_update_slice(inv, swap(shards[q], 1), ((low ^ q ^ 1) * own, 0))
        for b in rest:
            r = r + swap(r.astype(BF), b).astype(F32)
        pt = dot(r.astype(BF), inv, 1, 1).astype(BF)
        for b in rest:
            other = swap(pt, b)
            up = (me // b) % 2
            pt = jnp.where(up == 1, jnp.concatenate([other, pt], 1), jnp.concatenate([pt, other], 1))
        p = {0: pt}
        p[2] = swap(pt, 2)
        p[4] = swap(pt, 4)
        p[6] = swap(p[4], 2)
        for g in (0, 4, 2, 6):
            p[g ^ 1] = swap(p[g], 1)
        left = jnp.concatenate([cols(saved_solution, q) for q in range(8)], axis=1)
        grad = -dot(left, jnp.concatenate([p[q] for q in range(8)], axis=0), 1, 0)
        adj = jnp.zeros((own, sides), BF)
        for q in range(8):
            mine = lax.dynamic_slice(p[q], (0, me * own), (w, own)).T
            adj = lax.dynamic_update_slice(adj, mine, (0, (low ^ q) * w))
        return adj, grad.astype(BF)

    return body


def solution(mesh):
    n = mesh.shape["rows"]
    placed = P(("groups", "rows"), None)
    return jax.shard_map(
        make_tiled(n) if n == 16 else make_body(n),
        mesh=mesh,
        in_specs=(placed,) * 5,
        out_specs=(placed, placed),
        check_vma=False,
    )
```

profile of v0, /device:TPU:0, one launch (start us, length us, event | category | flops | bytes accessed | tf_op | source)
XLA Modules:
  0.0 130.4 jit_solution(1011190692479877212)
XLA Ops:
  0.8 5.9 %first.1 = (f32[64,2048]{1,0:T(8,128)S(1)}, bf16[64,2048]{1,0:T(8,128)(2,1)S(1)}, f32[64,2048]{1,0:T(8,128)S(1)}, bf16[64,2048]{1,0:T(8,128)(2,1)S(1)}, f32[64,2...) custom-call(s32[3]{0:T(128)S(1)} %pad_add_fusion.ids, ...), custom_call_target="tpu_custom_call" | custom-call | flops 2147483648 | bytes 8388608 | tf_op jit(solution)/shard_map/first/pallas_call | solution.py:115
  7.4 3.9 %shard_map.69 = (f32[64,2048]{1,0:T(8,128)S(1)}, bf16[64,2048]{1,0:T(8,128)(2,1)S(1)}, f32[64,2048]{1,0:T(8,128)S(1)}, bf16[64,2048]{1,0:T(8,128)(2,1)S(1)}, f32...) custom-call(s32[3]{0:T(128)S(1)} %pad_add_fusion.ids, ...), custom_call_target="tpu_custom_call" | custom-call | flops 2147483648 | bytes 10485760 | tf_op jit(solution)/shard_map/pallas_call | solution.py:173
  11.8 3.0 %collective-permute-start.9 = (bf16[128,2048]{1,0:T(8,128)(2,1)S(1)}, bf16[128,2048]{1,0:T(8,128)(2,1)S(1)}, u32[]{:S(2)}, u32[]{:S(2)}) collective-permute-start(bf16[128,2048]{1,0:T(8,128)(2,1)S(1)} %copy-done), channel_id=1, source_target_pairs={{0,4},{1,5},{2,6},{3,7},{4,0},{5,1},{6,2},{7,3},{8,12},{9,13},{10,... | collective-permute-start | bytes 1572872 | tf_op jit(solution)/shard_map/ppermute | solution.py:330
  20.2 6.8 %collective-permute-done.9.refs_2_ = bf16[128,2048]{1,0:T(8,128)(2,1)S(1)} collective-permute-done((bf16[128,2048]{1,0:T(8,128)(2,1)S(1)}, bf16[128,2048]{1,0:T(8,128)(2,1)S(1)}, u32[]{:S(2)}, u32[]{:S(2)}) %collective-permute-start.9) | collective-permute-done | bytes 524320 | tf_op jit(solution)/shard_map/ppermute | solution.py:330
  31.0 10.8 %collective-permute-done.5 = bf16[64,2048]{1,0:T(8,128)(2,1)S(1)} collective-permute-done((bf16[64,2048]{1,0:T(8,128)(2,1)S(1)}, bf16[64,2048]{1,0:T(8,128)(2,1)S(1)}, u32[]{:S(2)}, u32[]{:S(2)}) %collective-permute-start.5) | collective-permute-done | bytes 262176 | tf_op jit(solution)/shard_map/ppermute | solution.py:330
  45.9 2.9 %collective-permute-done.30 = bf16[64,2048]{1,0:T(8,128)(2,1)S(1)} collective-permute-done((bf16[64,2048]{1,0:T(8,128)(2,1)S(1)}, bf16[64,2048]{1,0:T(8,128)(2,1)S(1)}, u32[]{:S(2)}, u32[]{:S(2)}) %collective-permute-start.30) | collective-permute-done | bytes 262176 | tf_op jit(solution)/shard_map/ppermute | solution.py:330
  48.9 2.5 %collective-permute-start.6 = (bf16[64,2048]{1,0:T(8,128)(2,1)S(1)}, bf16[64,2048]{1,0:T(8,128)(2,1)S(1)}, u32[]{:S(2)}, u32[]{:S(2)}) collective-permute-start(bf16[64,2048]{1,0:T(8,128)(2,1)S(1)} %add_convert_fusion.5), channel_id=1, source_target_pairs={{0,4},{1,5},{2,6},{3,7},{4,0},{5,1},{6,2},{7,3},{8,12},{9,13},{10,... | collective-permute-start | bytes 786440 | tf_op jit(solution)/shard_map/ppermute | solution.py:330
  51.6 2.9 %collective-permute-done.15.refs_8_ = bf16[64,2048]{1,0:T(8,128)(2,1)S(1)} collective-permute-done((bf16[64,2048]{1,0:T(8,128)(2,1)S(1)}, bf16[64,2048]{1,0:T(8,128)(2,1)S(1)}, u32[]{:S(2)}, u32[]{:S(2)}) %collective-permute-start.15) | collective-permute-done | bytes 262176 | tf_op jit(solution)/shard_map/ppermute | solution.py:330
  54.5 2.6 %collective-permute-start.17 = (bf16[64,2048]{1,0:T(8,128)(2,1)S(1)}, bf16[64,2048]{1,0:T(8,128)(2,1)S(1)}, u32[]{:S(2)}, u32[]{:S(2)}) collective-permute-start(bf16[64,2048]{1,0:T(8,128)(2,1)S(1)} %slice.13), channel_id=1, source_target_pairs={{0,2},{1,3},{2,0},{3,1},{4,6},{5,7},{6,4},{7,5},{8,10},{9,11},{10,... | collective-permute-start | bytes 786440 | tf_op jit(solution)/shard_map/ppermute | solution.py:330
  57.3 2.1 %collective-permute-done.6 = bf16[64,2048]{1,0:T(8,128)(2,1)S(1)} collective-permute-done((bf16[64,2048]{1,0:T(8,128)(2,1)S(1)}, bf16[64,2048]{1,0:T(8,128)(2,1)S(1)}, u32[]{:S(2)}, u32[]{:S(2)}) %collective-permute-start.6) | collective-permute-done | bytes 262176 | tf_op jit(solution)/shard_map/ppermute | solution.py:330
  59.4 2.7 %collective-permute-start.31 = (bf16[64,2048]{1,0:T(8,128)(2,1)S(1)}, bf16[64,2048]{1,0:T(8,128)(2,1)S(1)}, u32[]{:S(2)}, u32[]{:S(2)}) collective-permute-start(bf16[64,2048]{1,0:T(8,128)(2,1)S(1)} %fusion.1), channel_id=1, source_target_pairs={{0,8},{1,9},{2,10},{3,11},{4,12},{5,13},{6,14},{7,15},{8,0},{9,1},... | collective-permute-start | bytes 786440 | tf_op jit(solution)/shard_map/ppermute | solution.py:330
  64.1 2.4 %collective-permute-start.7 = (bf16[64,2048]{1,0:T(8,128)(2,1)S(1)}, bf16[64,2048]{1,0:T(8,128)(2,1)S(1)}, u32[]{:S(2)}, u32[]{:S(2)}) collective-permute-start(bf16[64,2048]{1,0:T(8,128)(2,1)S(1)} %fusion), channel_id=1, source_target_pairs={{0,8},{1,9},{2,10},{3,11},{4,12},{5,13},{6,14},{7,15},{8,0},{9,1},... | collective-permute-start | bytes 786440 | tf_op jit(solution)/shard_map/ppermute | solution.py:330
  66.5 13.5 %collective-permute-done.31 = bf16[64,2048]{1,0:T(8,128)(2,1)S(1)} collective-permute-done((bf16[64,2048]{1,0:T(8,128)(2,1)S(1)}, bf16[64,2048]{1,0:T(8,128)(2,1)S(1)}, u32[]{:S(2)}, u32[]{:S(2)}) %collective-permute-start.31) | collective-permute-done | bytes 262176 | tf_op jit(solution)/shard_map/ppermute | solution.py:330
  85.2 1.9 %shard_map.71 = bf16[64,1024]{1,0:T(8,128)(2,1)S(1)} custom-call(s32[3]{0:T(128)S(1)} %pad_add_fusion.ids, bf16[64,2048]{1,0:T(8,128)(2,1)S(1)} %add_convert_fusion.4.r, bf16[1024,2048]{1,0:T(8,128)(2,1)S(1)} %shard_map.70.inv), custom_call_target="tpu_custom_call" | custom-call | flops 268435456 | bytes 4194304 | tf_op jit(solution)/shard_map/pallas_call | solution.py:237
  87.1 2.3 %collective-permute-start.19 = (bf16[64,1024]{1,0:T(8,128)(2,1)S(1)}, bf16[64,1024]{1,0:T(8,128)(2,1)S(1)}, u32[]{:S(2)}, u32[]{:S(2)}) collective-permute-start(bf16[64,1024]{1,0:T(8,128)(2,1)S(1)} %shard_map.71), channel_id=1, source_target_pairs={{0,8},{1,9},{2,10},{3,11},{4,12},{5,13},{6,14},{7,15},{8,0},{9,1},... | collective-permute-start | bytes 393224 | tf_op jit(solution)/shard_map/ppermute | solution.py:330
  89.4 7.5 %collective-permute-done.32 = bf16[64,1024]{1,0:T(8,128)(2,1)S(1)} collective-permute-done((bf16[64,1024]{1,0:T(8,128)(2,1)S(1)}, bf16[64,1024]{1,0:T(8,128)(2,1)S(1)}, u32[]{:S(2)}, u32[]{:S(2)}) %collective-permute-start.32) | collective-permute-done | bytes 131104 | tf_op jit(solution)/shard_map/ppermute | solution.py:330
  101.2 5.0 %collective-permute-done.33.refs_0_.refs_2_ = bf16[64,2048]{1,0:T(8,128)(2,1)S(1)} collective-permute-done((bf16[64,2048]{1,0:T(8,128)(2,1)S(1)}, bf16[64,2048]{1,0:T(8,128)(2,1)S(1)}, u32[]{:S(2)}, u32[]{:S(2)}) %collective-permute-start.33) | collective-permute-done | bytes 262176 | tf_op jit(solution)/shard_map/ppermute | solution.py:330
  108.3 3.6 %collective-permute-done.20.refs_0_.refs_10_ = bf16[64,2048]{1,0:T(8,128)(2,1)S(1)} collective-permute-done((bf16[64,2048]{1,0:T(8,128)(2,1)S(1)}, bf16[64,2048]{1,0:T(8,128)(2,1)S(1)}, u32[]{:S(2)}, u32[]{:S(2)}) %collective-permute-start.20) | collective-permute-done | bytes 262176 | tf_op jit(solution)/shard_map/ppermute | solution.py:330
  112.5 2.2 %shard_map.68.s = bf16[1024,1024]{1,0:T(8,128)(2,1)S(1)} custom-call(s32[3]{0:T(128)S(1)} %pad_add_fusion.ids, bf16[1024,1024]{1,0:T(8,128)(2,1)S(1)} %copy-done.1), custom_call_target="tpu_custom_call" | custom-call | bytes 4194304 | tf_op jit(solution)/shard_map/pallas_call | solution.py:196
  114.7 2.2 %collective-permute-done.39.refs_6_ = bf16[64,2048]{1,0:T(8,128)(2,1)S(1)} collective-permute-done((bf16[64,2048]{1,0:T(8,128)(2,1)S(1)}, bf16[64,2048]{1,0:T(8,128)(2,1)S(1)}, u32[]{:S(2)}, u32[]{:S(2)}) %collective-permute-start.39) | collective-permute-done | bytes 262176 | tf_op jit(solution)/shard_map/ppermute | solution.py:330
  117.0 2.2 %collective-permute-done.41.refs_14_ = bf16[64,2048]{1,0:T(8,128)(2,1)S(1)} collective-permute-done((bf16[64,2048]{1,0:T(8,128)(2,1)S(1)}, bf16[64,2048]{1,0:T(8,128)(2,1)S(1)}, u32[]{:S(2)}, u32[]{:S(2)}) %collective-permute-start.41) | collective-permute-done | bytes 262176 | tf_op jit(solution)/shard_map/ppermute | solution.py:330
  120.9 2.7 %shard_map.74.refs_4_ = f32[1024,2048]{1,0:T(8,128)S(1)} custom-call(s32[3]{0:T(128)S(1)} %pad_add_fusion.ids, bf16[1024,1024]{1,0:T(8,128)(2,1)S(1)} %shard_map.68.s, bf16[64,2048]{1,0:T(8,128)(2,1)S(1)} %collective-permute-done.33.refs_0_.refs_2_, bf16[64,2048]{1,0:T(8,128)(2,1)S(1)} %collective-permute-done.34.refs_1_.refs_3_, ...), custom_call_target="tpu_custom_call", output_to_operand_aliasing={{}: (6, {})} | custom-call | flops 1073741824 | bytes 8388608 | tf_op jit(solution)/shard_map/pallas_call | solution.py:269
  123.7 2.7 %shard_map.75.acc = f32[1024,2048]{1,0:T(8,128)S(1)} custom-call(s32[3]{0:T(128)S(1)} %pad_add_fusion.ids, bf16[1024,1024]{1,0:T(8,128)(2,1)S(1)} %shard_map.68.s, bf16[64,2048]{1,0:T(8,128)(2,1)S(1)} %collective-permute-done.20.refs_0_.refs_10_, bf16[64,2048]{1,0:T(8,128)(2,1)S(1)} %collective-permute-done.21.refs_1_.refs_11_, ...), custom_call_target="tpu_custom_call", output_to_operand_aliasing={{}: (6, {})} | custom-call | flops 1073741824 | bytes 8388608 | tf_op jit(solution)/shard_map/pallas_call | solution.py:269
  126.5 3.7 %last.1 = (bf16[1024,2048]{1,0:T(8,128)(2,1)}, bf16[128,1024]{1,0:T(8,128)(2,1)}) custom-call(s32[3]{0:T(128)S(1)} %pad_add_fusion.ids, bf16[1024,1024]{1,0:T(8,128)(2,1)S(1)} %shard_map.68.s, f32[1024,2048]{1,0:T(8,128)S(1)} %shard_map.75.acc, bf16[64,2048]{1,0:T(8,128)(2,1)S(1)} %pad_maximum_fusion.1.refs_0_, ...), custom_call_target="tpu_custom_call" | custom-call | flops 1073741824 | bytes 8388608 | tf_op jit(solution)/shard_map/last/pallas_call | solution.py:309
  (98 shorter events, 31.0 us)
Async XLA Ops:
  7.3 21.4 %collective-permute-start.27 = (bf16[64,2048]{1,0:T(8,128)(2,1)S(1)}, bf16[64,2048]{1,0:T(8,128)(2,1)S(1)}, u32[]{:S(2)}, u32[]{:S(2)}) collective-permute-start(bf16[64,2048]{1,0:T(8,128)(2,1)S(1)} %get-tuple-element.33), channel_id=1, source_target_pairs={{0,1},{1,0},{2,3},{3,2},{4,5},{5,4},{6,7},{7,6},{8,9},{9,8},{10,11... | collective-permute-start | bytes 786440 | tf_op jit(solution)/shard_map/ppermute | solution.py:330
  11.7 31.9 %collective-permute-start.24 = (bf16[64,2048]{1,0:T(8,128)(2,1)S(1)}, bf16[64,2048]{1,0:T(8,128)(2,1)S(1)}, u32[]{:S(2)}, u32[]{:S(2)}) collective-permute-start(bf16[64,2048]{1,0:T(8,128)(2,1)S(1)} %get-tuple-element.29), channel_id=1, source_target_pairs={{0,1},{1,0},{2,3},{3,2},{4,5},{5,4},{6,7},{7,6},{8,9},{9,8},{10,11... | collective-permute-start | bytes 786440 | tf_op jit(solution)/shard_map/ppermute | solution.py:330
  11.8 15.2 %collective-permute-start.9 = (bf16[128,2048]{1,0:T(8,128)(2,1)S(1)}, bf16[128,2048]{1,0:T(8,128)(2,1)S(1)}, u32[]{:S(2)}, u32[]{:S(2)}) collective-permute-start(bf16[128,2048]{1,0:T(8,128)(2,1)S(1)} %copy-done), channel_id=1, source_target_pairs={{0,4},{1,5},{2,6},{3,7},{4,0},{5,1},{6,2},{7,3},{8,12},{9,13},{10,... | collective-permute-start | bytes 1572872 | tf_op jit(solution)/shard_map/ppermute | solution.py:330
  14.9 28.8 %collective-permute-start.11 = (bf16[64,2048]{1,0:T(8,128)(2,1)S(1)}, bf16[64,2048]{1,0:T(8,128)(2,1)S(1)}, u32[]{:S(2)}, u32[]{:S(2)}) collective-permute-start(bf16[64,2048]{1,0:T(8,128)(2,1)S(1)} %slice.9), channel_id=1, source_target_pairs={{0,2},{1,3},{2,0},{3,1},{4,6},{5,7},{6,4},{7,5},{8,10},{9,11},{10,... | collective-permute-start | bytes 786440 | tf_op jit(solution)/shard_map/ppermute | solution.py:330
  27.0 18.3 %collective-permute-start.13 = (bf16[64,2048]{1,0:T(8,128)(2,1)S(1)}, bf16[64,2048]{1,0:T(8,128)(2,1)S(1)}, u32[]{:S(2)}, u32[]{:S(2)}) collective-permute-start(bf16[64,2048]{1,0:T(8,128)(2,1)S(1)} %slice.12), channel_id=1, source_target_pairs={{0,2},{1,3},{2,0},{3,1},{4,6},{5,7},{6,4},{7,5},{8,10},{9,11},{10,... | collective-permute-start | bytes 786440 | tf_op jit(solution)/shard_map/ppermute | solution.py:330
  28.7 13.0 %collective-permute-start.5 = (bf16[64,2048]{1,0:T(8,128)(2,1)S(1)}, bf16[64,2048]{1,0:T(8,128)(2,1)S(1)}, u32[]{:S(2)}, u32[]{:S(2)}) collective-permute-start(bf16[64,2048]{1,0:T(8,128)(2,1)S(1)} %add_convert_fusion.6), channel_id=1, source_target_pairs={{0,2},{1,3},{2,0},{3,1},{4,6},{5,7},{6,4},{7,5},{8,10},{9,11},{10,... | collective-permute-start | bytes 786440 | tf_op jit(solution)/shard_map/ppermute | solution.py:330
  30.3 15.7 %collective-permute-start.26 = (bf16[64,2048]{1,0:T(8,128)(2,1)S(1)}, bf16[64,2048]{1,0:T(8,128)(2,1)S(1)}, u32[]{:S(2)}, u32[]{:S(2)}) collective-permute-start(bf16[64,2048]{1,0:T(8,128)(2,1)S(1)} %add_convert_fusion.3), channel_id=1, source_target_pairs={{0,2},{1,3},{2,0},{3,1},{4,6},{5,7},{6,4},{7,5},{8,10},{9,11},{10,... | collective-permute-start | bytes 786440 | tf_op jit(solution)/shard_map/ppermute | solution.py:330
  43.7 13.4 %collective-permute-start.2 = (bf16[64,2048]{1,0:T(8,128)(2,1)S(1)}, bf16[64,2048]{1,0:T(8,128)(2,1)S(1)}, u32[]{:S(2)}, u32[]{:S(2)}) collective-permute-start(bf16[64,2048]{1,0:T(8,128)(2,1)S(1)} %add_convert_fusion.7), channel_id=1, source_target_pairs={{0,2},{1,3},{2,0},{3,1},{4,6},{5,7},{6,4},{7,5},{8,10},{9,11},{10,... | collective-permute-start | bytes 786440 | tf_op jit(solution)/shard_map/ppermute | solution.py:330
  48.9 10.5 %collective-permute-start.6 = (bf16[64,2048]{1,0:T(8,128)(2,1)S(1)}, bf16[64,2048]{1,0:T(8,128)(2,1)S(1)}, u32[]{:S(2)}, u32[]{:S(2)}) collective-permute-start(bf16[64,2048]{1,0:T(8,128)(2,1)S(1)} %add_convert_fusion.5), channel_id=1, source_target_pairs={{0,4},{1,5},{2,6},{3,7},{4,0},{5,1},{6,2},{7,3},{8,12},{9,13},{10,... | collective-permute-start | bytes 786440 | tf_op jit(solution)/shard_map/ppermute | solution.py:330
  51.5 28.7 %collective-permute-start.8 = (bf16[128,2048]{1,0:T(8,128)(2,1)S(1)}, bf16[128,2048]{1,0:T(8,128)(2,1)S(1)}, u32[]{:S(2)}, u32[]{:S(2)}) collective-permute-start(bf16[128,2048]{1,0:T(8,128)(2,1)S(1)} %copy-done), channel_id=1, source_target_pairs={{0,1},{1,0},{2,3},{3,2},{4,5},{5,4},{6,7},{7,6},{8,9},{9,8},{10,11... | collective-permute-start | bytes 1572872 | tf_op jit(solution)/shard_map/ppermute | solution.py:330
  54.5 9.6 %collective-permute-start.17 = (bf16[64,2048]{1,0:T(8,128)(2,1)S(1)}, bf16[64,2048]{1,0:T(8,128)(2,1)S(1)}, u32[]{:S(2)}, u32[]{:S(2)}) collective-permute-start(bf16[64,2048]{1,0:T(8,128)(2,1)S(1)} %slice.13), channel_id=1, source_target_pairs={{0,2},{1,3},{2,0},{3,1},{4,6},{5,7},{6,4},{7,5},{8,10},{9,11},{10,... | collective-permute-start | bytes 786440 | tf_op jit(solution)/shard_map/ppermute | solution.py:330
  57.1 24.4 %collective-permute-start.10 = (bf16[128,2048]{1,0:T(8,128)(2,1)S(1)}, bf16[128,2048]{1,0:T(8,128)(2,1)S(1)}, u32[]{:S(2)}, u32[]{:S(2)}) collective-permute-start(bf16[128,2048]{1,0:T(8,128)(2,1)S(1)} %collective-permute-done.9.refs_2_), channel_id=1, source_target_pairs={{0,1},{1,0},{2,3},{3,2},{4,5},{5,4},{6,7},{7,6},{8,9},{9,8},{10,11... | collective-permute-start | bytes 1572872 | tf_op jit(solution)/shard_map/ppermute | solution.py:330
  59.4 20.6 %collective-permute-start.31 = (bf16[64,2048]{1,0:T(8,128)(2,1)S(1)}, bf16[64,2048]{1,0:T(8,128)(2,1)S(1)}, u32[]{:S(2)}, u32[]{:S(2)}) collective-permute-start(bf16[64,2048]{1,0:T(8,128)(2,1)S(1)} %fusion.1), channel_id=1, source_target_pairs={{0,8},{1,9},{2,10},{3,11},{4,12},{5,13},{6,14},{7,15},{8,0},{9,1},... | collective-permute-start | bytes 786440 | tf_op jit(solution)/shard_map/ppermute | solution.py:330
  62.3 17.9 %collective-permute-start.16 = (bf16[64,2048]{1,0:T(8,128)(2,1)S(1)}, bf16[64,2048]{1,0:T(8,128)(2,1)S(1)}, u32[]{:S(2)}, u32[]{:S(2)}) collective-permute-start(bf16[64,2048]{1,0:T(8,128)(2,1)S(1)} %collective-permute-done.15.refs_8_), channel_id=1, source_target_pairs={{0,1},{1,0},{2,3},{3,2},{4,5},{5,4},{6,7},{7,6},{8,9},{9,8},{10,11... | collective-permute-start | bytes 786440 | tf_op jit(solution)/shard_map/ppermute | solution.py:330
  64.1 21.0 %collective-permute-start.7 = (bf16[64,2048]{1,0:T(8,128)(2,1)S(1)}, bf16[64,2048]{1,0:T(8,128)(2,1)S(1)}, u32[]{:S(2)}, u32[]{:S(2)}) collective-permute-start(bf16[64,2048]{1,0:T(8,128)(2,1)S(1)} %fusion), channel_id=1, source_target_pairs={{0,8},{1,9},{2,10},{3,11},{4,12},{5,13},{6,14},{7,15},{8,0},{9,1},... | collective-permute-start | bytes 786440 | tf_op jit(solution)/shard_map/ppermute | solution.py:330
  84.3 12.7 %collective-permute-start.32 = (bf16[64,1024]{1,0:T(8,128)(2,1)S(1)}, bf16[64,1024]{1,0:T(8,128)(2,1)S(1)}, u32[]{:S(2)}, u32[]{:S(2)}) collective-permute-start(bf16[64,1024]{1,0:T(8,128)(2,1)S(1)} %shard_map.72), channel_id=1, source_target_pairs={{0,8},{1,9},{2,10},{3,11},{4,12},{5,13},{6,14},{7,15},{8,0},{9,1},... | collective-permute-start | bytes 393224 | tf_op jit(solution)/shard_map/ppermute | solution.py:330
  87.1 12.1 %collective-permute-start.19 = (bf16[64,1024]{1,0:T(8,128)(2,1)S(1)}, bf16[64,1024]{1,0:T(8,128)(2,1)S(1)}, u32[]{:S(2)}, u32[]{:S(2)}) collective-permute-start(bf16[64,1024]{1,0:T(8,128)(2,1)S(1)} %shard_map.71), channel_id=1, source_target_pairs={{0,8},{1,9},{2,10},{3,11},{4,12},{5,13},{6,14},{7,15},{8,0},{9,1},... | collective-permute-start | bytes 393224 | tf_op jit(solution)/shard_map/ppermute | solution.py:330
  99.2 12.7 %collective-permute-start.20 = (bf16[64,2048]{1,0:T(8,128)(2,1)S(1)}, bf16[64,2048]{1,0:T(8,128)(2,1)S(1)}, u32[]{:S(2)}, u32[]{:S(2)}) collective-permute-start(bf16[64,2048]{1,0:T(8,128)(2,1)S(1)} %pad_maximum_fusion.refs_2_.refs_8_), channel_id=1, source_target_pairs={{0,2},{1,3},{2,0},{3,1},{4,6},{5,7},{6,4},{7,5},{8,10},{9,11},{10,... | collective-permute-start | bytes 786440 | tf_op jit(solution)/shard_map/ppermute | solution.py:330
  99.5 12.4 %collective-permute-start.38 = (bf16[64,2048]{1,0:T(8,128)(2,1)S(1)}, bf16[64,2048]{1,0:T(8,128)(2,1)S(1)}, u32[]{:S(2)}, u32[]{:S(2)}) collective-permute-start(bf16[64,2048]{1,0:T(8,128)(2,1)S(1)} %pad_maximum_fusion.refs_2_.refs_8_), channel_id=1, source_target_pairs={{0,1},{1,0},{2,3},{3,2},{4,5},{5,4},{6,7},{7,6},{8,9},{9,8},{10,11... | collective-permute-start | bytes 786440 | tf_op jit(solution)/shard_map/ppermute | solution.py:330
  99.5 12.4 %collective-permute-start.22 = (bf16[64,2048]{1,0:T(8,128)(2,1)S(1)}, bf16[64,2048]{1,0:T(8,128)(2,1)S(1)}, u32[]{:S(2)}, u32[]{:S(2)}) collective-permute-start(bf16[64,2048]{1,0:T(8,128)(2,1)S(1)} %pad_maximum_fusion.refs_2_.refs_8_), channel_id=1, source_target_pairs={{0,4},{1,5},{2,6},{3,7},{4,0},{5,1},{6,2},{7,3},{8,12},{9,13},{10,... | collective-permute-start | bytes 786440 | tf_op jit(solution)/shard_map/ppermute | solution.py:330
  106.7 10.2 %collective-permute-start.39 = (bf16[64,2048]{1,0:T(8,128)(2,1)S(1)}, bf16[64,2048]{1,0:T(8,128)(2,1)S(1)}, u32[]{:S(2)}, u32[]{:S(2)}) collective-permute-start(bf16[64,2048]{1,0:T(8,128)(2,1)S(1)} %collective-permute-done.35.refs_2_.refs_4_), channel_id=1, source_target_pairs={{0,2},{1,3},{2,0},{3,1},{4,6},{5,7},{6,4},{7,5},{8,10},{9,11},{10,... | collective-permute-start | bytes 786440 | tf_op jit(solution)/shard_map/ppermute | solution.py:330
  111.9 11.8 %collective-permute-start.21 = (bf16[64,2048]{1,0:T(8,128)(2,1)S(1)}, bf16[64,2048]{1,0:T(8,128)(2,1)S(1)}, u32[]{:S(2)}, u32[]{:S(2)}) collective-permute-start(bf16[64,2048]{1,0:T(8,128)(2,1)S(1)} %collective-permute-done.20.refs_0_.refs_10_), channel_id=1, source_target_pairs={{0,1},{1,0},{2,3},{3,2},{4,5},{5,4},{6,7},{7,6},{8,9},{9,8},{10,11... | collective-permute-start | bytes 786440 | tf_op jit(solution)/shard_map/ppermute | solution.py:330
  112.4 11.3 %collective-permute-start.23 = (bf16[64,2048]{1,0:T(8,128)(2,1)S(1)}, bf16[64,2048]{1,0:T(8,128)(2,1)S(1)}, u32[]{:S(2)}, u32[]{:S(2)}) collective-permute-start(bf16[64,2048]{1,0:T(8,128)(2,1)S(1)} %collective-permute-done.22.refs_2_.refs_12_), channel_id=1, source_target_pairs={{0,1},{1,0},{2,3},{3,2},{4,5},{5,4},{6,7},{7,6},{8,9},{9,8},{10,11... | collective-permute-start | bytes 786440 | tf_op jit(solution)/shard_map/ppermute | solution.py:330
  117.0 9.5 %collective-permute-start.40 = (bf16[64,2048]{1,0:T(8,128)(2,1)S(1)}, bf16[64,2048]{1,0:T(8,128)(2,1)S(1)}, u32[]{:S(2)}, u32[]{:S(2)}) collective-permute-start(bf16[64,2048]{1,0:T(8,128)(2,1)S(1)} %collective-permute-done.39.refs_6_), channel_id=1, source_target_pairs={{0,1},{1,0},{2,3},{3,2},{4,5},{5,4},{6,7},{7,6},{8,9},{9,8},{10,11... | collective-permute-start | bytes 786440 | tf_op jit(solution)/shard_map/ppermute | solution.py:330
  (24 other events, 173.4 us)
where the time goes:
time: 131 us; the launch traced here: 130 us
  waiting for transfers between devices  68.5 us (52%)
  starting transfers between devices  31.9 us (24%)
  Pallas kernels  27.7 us (21%)
    ppermute x43, waiting for transfers between devices, swap(): return lax.ppermute(a, 'rows', [(i, i ^ bit) for i in range(n)])  68.5 us
    ppermute x43, starting transfers between devices, swap(): return lax.ppermute(a, 'rows', [(i, i ^ bit) for i in range(n)])  31.9 us
    pallas_call x3, Pallas kernels, outer(): once(functools.partial(outer_kernel, len(pieces), lo, acc is None), jax.S...  7.26 us
    pallas_call x1, Pallas kernels, first(): pl.pallas_call(functools.partial(first_kernel, groups), out_shape=shapes,...  5.94 us
    pallas_call x1, Pallas kernels, again(): once(functools.partial(again_kernel, groups), shapes, 3, [pltpu.VMEM((n *...  3.86 us
    pallas_call x2, Pallas kernels, middle(): call(middle_kernel, jax.ShapeDtypeStruct((m, n), BF), (1,), [pl.BlockSpec...  3.85 us
    pallas_call x1, Pallas kernels, last(): pl.pallas_call(functools.partial(last_kernel, n_in, lo), out_shape=(jax.S...  3.73 us
  transfers between devices with their start and end apart: 43, of which 20 were waited for; matrix products, arithmetic and copies ran while one was open for 1% of the time, Pallas kernels for 14%

commit v1 on v0

--- a/solution.py
+++ b/solution.py
@@ -318,6 +318,26 @@
     )(ids, saved, acc, *pieces)
 
 
+def upper_kernel(inv, out, sem):
+    copy = pltpu.make_async_copy(inv.at[:out.shape[0]], out, sem)
+    copy.start()
+    copy.wait()
+
+
+def upper(inverse):
+    rows, width = inverse.shape
+    return pl.pallas_call(
+        upper_kernel,
+        out_shape=jax.ShapeDtypeStruct((rows // 2, width), BF),
+        in_specs=[pl.BlockSpec(memory_space=pltpu.HBM)],
+        out_specs=WHOLE,
+        scratch_shapes=[pltpu.SemaphoreType.DMA(())],
+        compiler_params=pltpu.CompilerParams(vmem_limit_bytes=2 << 20),
+        cost_estimate=cost(0, rows * width),
+        name="upper",
+    )(pltpu.with_memory_space_constraint(inverse, pltpu.HBM))
+
+
 ORDER = (
     (0, 0), (0, 1), (1, 0), (1, 1), (0, 2), (0, 3), (0, 4), (0, 5),
     (1, 2), (1, 3), (1, 4), (1, 5), (0, 6), (0, 7), (1, 6), (1, 7),
@@ -336,7 +356,7 @@
 
         half = own // 2
         again_inverse = lax.optimization_barrier(inverse_block)
-        i2a = swap(inverse_block[:half], 2)
+        i2a = swap(upper(inverse_block), 2)
         i4 = swap(inverse_block, 4)
         i2b = swap(again_inverse[half:], 2)
         i6z = swap(i2a, 4)

time: 131 us -> 131 us (level)
  transfers between devices with their start and end apart: 43 -> 43, of which waited for: 20 -> 20; matrix products, arithmetic and copies ran while one was open for 1% -> 1% of each run, Pallas kernels for 14% -> 15%
where the time goes in v1:
time: 131 us; the launch traced here: 130 us
  waiting for transfers between devices  67.5 us (52%)
  starting transfers between devices  31.9 us (24%)
  Pallas kernels  28.7 us (22%)
    ppermute x43, waiting for transfers between devices, swap(): return lax.ppermute(a, 'rows', [(i, i ^ bit) for i in range(n)])  67.5 us
    ppermute x43, starting transfers between devices, swap(): return lax.ppermute(a, 'rows', [(i, i ^ bit) for i in range(n)])  31.9 us
    pallas_call x3, Pallas kernels, outer(): once(functools.partial(outer_kernel, len(pieces), lo, acc is None), jax.S...  7.26 us
    pallas_call x1, Pallas kernels, first(): pl.pallas_call(functools.partial(first_kernel, groups), out_shape=shapes,...  5.94 us
    pallas_call x1, Pallas kernels, again(): once(functools.partial(again_kernel, groups), shapes, 3, [pltpu.VMEM((n *...  3.86 us
    pallas_call x2, Pallas kernels, middle(): call(middle_kernel, jax.ShapeDtypeStruct((m, n), BF), (1,), [pl.BlockSpec...  3.85 us
    pallas_call x1, Pallas kernels, last(): pl.pallas_call(functools.partial(last_kernel, n_in, lo), out_shape=(jax.S...  3.73 us
  transfers between devices with their start and end apart: 43, of which 20 were waited for; matrix products, arithmetic and copies ran while one was open for 1% of the time, Pallas kernels for 15%

profile of v1, /device:TPU:0, one launch (start us, length us, event | category | flops | bytes accessed | tf_op | source)
XLA Modules:
  0.0 130.4 jit_solution(2100418086040150307)
XLA Ops:
  0.8 5.9 %first.1 = (f32[64,2048]{1,0:T(8,128)S(1)}, bf16[64,2048]{1,0:T(8,128)(2,1)S(1)}, f32[64,2048]{1,0:T(8,128)S(1)}, bf16[64,2048]{1,0:T(8,128)(2,1)S(1)}, f32[64,2...) custom-call(s32[3]{0:T(128)S(1)} %pad_add_fusion.ids, ...), custom_call_target="tpu_custom_call" | custom-call | flops 2147483648 | bytes 8388608 | tf_op jit(solution)/shard_map/first/pallas_call | solution.py:115
  7.4 3.9 %shard_map.69 = (f32[64,2048]{1,0:T(8,128)S(1)}, bf16[64,2048]{1,0:T(8,128)(2,1)S(1)}, f32[64,2048]{1,0:T(8,128)S(1)}, bf16[64,2048]{1,0:T(8,128)(2,1)S(1)}, f32...) custom-call(s32[3]{0:T(128)S(1)} %pad_add_fusion.ids, ...), custom_call_target="tpu_custom_call" | custom-call | flops 2147483648 | bytes 10485760 | tf_op jit(solution)/shard_map/pallas_call | solution.py:173
  11.8 3.0 %collective-permute-start.9 = (bf16[128,2048]{1,0:T(8,128)(2,1)S(1)}, bf16[128,2048]{1,0:T(8,128)(2,1)S(1)}, u32[]{:S(2)}, u32[]{:S(2)}) collective-permute-start(bf16[128,2048]{1,0:T(8,128)(2,1)S(1)} %copy-done), channel_id=1, source_target_pairs={{0,4},{1,5},{2,6},{3,7},{4,0},{5,1},{6,2},{7,3},{8,12},{9,13},{10,... | collective-permute-start | bytes 1572872 | tf_op jit(solution)/shard_map/ppermute | solution.py:350
  21.2 5.8 %collective-permute-done.9.refs_2_ = bf16[128,2048]{1,0:T(8,128)(2,1)S(1)} collective-permute-done((bf16[128,2048]{1,0:T(8,128)(2,1)S(1)}, bf16[128,2048]{1,0:T(8,128)(2,1)S(1)}, u32[]{:S(2)}, u32[]{:S(2)}) %collective-permute-start.9) | collective-permute-done | bytes 524320 | tf_op jit(solution)/shard_map/ppermute | solution.py:350
  32.2 9.6 %collective-permute-done.5 = bf16[64,2048]{1,0:T(8,128)(2,1)S(1)} collective-permute-done((bf16[64,2048]{1,0:T(8,128)(2,1)S(1)}, bf16[64,2048]{1,0:T(8,128)(2,1)S(1)}, u32[]{:S(2)}, u32[]{:S(2)}) %collective-permute-start.5) | collective-permute-done | bytes 262176 | tf_op jit(solution)/shard_map/ppermute | solution.py:350
  46.4 2.5 %collective-permute-done.30 = bf16[64,2048]{1,0:T(8,128)(2,1)S(1)} collective-permute-done((bf16[64,2048]{1,0:T(8,128)(2,1)S(1)}, bf16[64,2048]{1,0:T(8,128)(2,1)S(1)}, u32[]{:S(2)}, u32[]{:S(2)}) %collective-permute-start.30) | collective-permute-done | bytes 262176 | tf_op jit(solution)/shard_map/ppermute | solution.py:350
  48.9 2.5 %collective-permute-start.6 = (bf16[64,2048]{1,0:T(8,128)(2,1)S(1)}, bf16[64,2048]{1,0:T(8,128)(2,1)S(1)}, u32[]{:S(2)}, u32[]{:S(2)}) collective-permute-start(bf16[64,2048]{1,0:T(8,128)(2,1)S(1)} %add_convert_fusion.5), channel_id=1, source_target_pairs={{0,4},{1,5},{2,6},{3,7},{4,0},{5,1},{6,2},{7,3},{8,12},{9,13},{10,... | collective-permute-start | bytes 786440 | tf_op jit(solution)/shard_map/ppermute | solution.py:350
  51.6 2.9 %collective-permute-done.15.refs_8_ = bf16[64,2048]{1,0:T(8,128)(2,1)S(1)} collective-permute-done((bf16[64,2048]{1,0:T(8,128)(2,1)S(1)}, bf16[64,2048]{1,0:T(8,128)(2,1)S(1)}, u32[]{:S(2)}, u32[]{:S(2)}) %collective-permute-start.15) | collective-permute-done | bytes 262176 | tf_op jit(solution)/shard_map/ppermute | solution.py:350
  54.5 2.6 %collective-permute-start.17 = (bf16[64,2048]{1,0:T(8,128)(2,1)S(1)}, bf16[64,2048]{1,0:T(8,128)(2,1)S(1)}, u32[]{:S(2)}, u32[]{:S(2)}) collective-permute-start(bf16[64,2048]{1,0:T(8,128)(2,1)S(1)} %slice.9), channel_id=1, source_target_pairs={{0,2},{1,3},{2,0},{3,1},{4,6},{5,7},{6,4},{7,5},{8,10},{9,11},{10,... | collective-permute-start | bytes 786440 | tf_op jit(solution)/shard_map/ppermute | solution.py:350
  57.3 2.1 %collective-permute-done.6 = bf16[64,2048]{1,0:T(8,128)(2,1)S(1)} collective-permute-done((bf16[64,2048]{1,0:T(8,128)(2,1)S(1)}, bf16[64,2048]{1,0:T(8,128)(2,1)S(1)}, u32[]{:S(2)}, u32[]{:S(2)}) %collective-permute-start.6) | collective-permute-done | bytes 262176 | tf_op jit(solution)/shard_map/ppermute | solution.py:350
  59.4 2.7 %collective-permute-start.31 = (bf16[64,2048]{1,0:T(8,128)(2,1)S(1)}, bf16[64,2048]{1,0:T(8,128)(2,1)S(1)}, u32[]{:S(2)}, u32[]{:S(2)}) collective-permute-start(bf16[64,2048]{1,0:T(8,128)(2,1)S(1)} %fusion.1), channel_id=1, source_target_pairs={{0,8},{1,9},{2,10},{3,11},{4,12},{5,13},{6,14},{7,15},{8,0},{9,1},... | collective-permute-start | bytes 786440 | tf_op jit(solution)/shard_map/ppermute | solution.py:350
  64.1 2.4 %collective-permute-start.7 = (bf16[64,2048]{1,0:T(8,128)(2,1)S(1)}, bf16[64,2048]{1,0:T(8,128)(2,1)S(1)}, u32[]{:S(2)}, u32[]{:S(2)}) collective-permute-start(bf16[64,2048]{1,0:T(8,128)(2,1)S(1)} %fusion), channel_id=1, source_target_pairs={{0,8},{1,9},{2,10},{3,11},{4,12},{5,13},{6,14},{7,15},{8,0},{9,1},... | collective-permute-start | bytes 786440 | tf_op jit(solution)/shard_map/ppermute | solution.py:350
  66.5 13.5 %collective-permute-done.31 = bf16[64,2048]{1,0:T(8,128)(2,1)S(1)} collective-permute-done((bf16[64,2048]{1,0:T(8,128)(2,1)S(1)}, bf16[64,2048]{1,0:T(8,128)(2,1)S(1)}, u32[]{:S(2)}, u32[]{:S(2)}) %collective-permute-start.31) | collective-permute-done | bytes 262176 | tf_op jit(solution)/shard_map/ppermute | solution.py:350
  85.2 1.9 %shard_map.71 = bf16[64,1024]{1,0:T(8,128)(2,1)S(1)} custom-call(s32[3]{0:T(128)S(1)} %pad_add_fusion.ids, bf16[64,2048]{1,0:T(8,128)(2,1)S(1)} %add_convert_fusion.4.r, bf16[1024,2048]{1,0:T(8,128)(2,1)S(1)} %shard_map.70.inv), custom_call_target="tpu_custom_call" | custom-call | flops 268435456 | bytes 4194304 | tf_op jit(solution)/shard_map/pallas_call | solution.py:237
  87.1 2.3 %collective-permute-start.19 = (bf16[64,1024]{1,0:T(8,128)(2,1)S(1)}, bf16[64,1024]{1,0:T(8,128)(2,1)S(1)}, u32[]{:S(2)}, u32[]{:S(2)}) collective-permute-start(bf16[64,1024]{1,0:T(8,128)(2,1)S(1)} %shard_map.71), channel_id=1, source_target_pairs={{0,8},{1,9},{2,10},{3,11},{4,12},{5,13},{6,14},{7,15},{8,0},{9,1},... | collective-permute-start | bytes 393224 | tf_op jit(solution)/shard_map/ppermute | solution.py:350
  89.4 7.5 %collective-permute-done.32 = bf16[64,1024]{1,0:T(8,128)(2,1)S(1)} collective-permute-done((bf16[64,1024]{1,0:T(8,128)(2,1)S(1)}, bf16[64,1024]{1,0:T(8,128)(2,1)S(1)}, u32[]{:S(2)}, u32[]{:S(2)}) %collective-permute-start.32) | collective-permute-done | bytes 131104 | tf_op jit(solution)/shard_map/ppermute | solution.py:350
  101.3 5.0 %collective-permute-done.33.refs_0_.refs_2_ = bf16[64,2048]{1,0:T(8,128)(2,1)S(1)} collective-permute-done((bf16[64,2048]{1,0:T(8,128)(2,1)S(1)}, bf16[64,2048]{1,0:T(8,128)(2,1)S(1)}, u32[]{:S(2)}, u32[]{:S(2)}) %collective-permute-start.33) | collective-permute-done | bytes 262176 | tf_op jit(solution)/shard_map/ppermute | solution.py:350
  108.3 3.6 %collective-permute-done.20.refs_0_.refs_10_ = bf16[64,2048]{1,0:T(8,128)(2,1)S(1)} collective-permute-done((bf16[64,2048]{1,0:T(8,128)(2,1)S(1)}, bf16[64,2048]{1,0:T(8,128)(2,1)S(1)}, u32[]{:S(2)}, u32[]{:S(2)}) %collective-permute-start.20) | collective-permute-done | bytes 262176 | tf_op jit(solution)/shard_map/ppermute | solution.py:350
  112.5 2.2 %shard_map.68.s = bf16[1024,1024]{1,0:T(8,128)(2,1)S(1)} custom-call(s32[3]{0:T(128)S(1)} %pad_add_fusion.ids, bf16[1024,1024]{1,0:T(8,128)(2,1)S(1)} %copy-done.2), custom_call_target="tpu_custom_call" | custom-call | bytes 4194304 | tf_op jit(solution)/shard_map/pallas_call | solution.py:196
  114.8 2.2 %collective-permute-done.39.refs_6_ = bf16[64,2048]{1,0:T(8,128)(2,1)S(1)} collective-permute-done((bf16[64,2048]{1,0:T(8,128)(2,1)S(1)}, bf16[64,2048]{1,0:T(8,128)(2,1)S(1)}, u32[]{:S(2)}, u32[]{:S(2)}) %collective-permute-start.39) | collective-permute-done | bytes 262176 | tf_op jit(solution)/shard_map/ppermute | solution.py:350
  117.0 2.2 %collective-permute-done.41.refs_14_ = bf16[64,2048]{1,0:T(8,128)(2,1)S(1)} collective-permute-done((bf16[64,2048]{1,0:T(8,128)(2,1)S(1)}, bf16[64,2048]{1,0:T(8,128)(2,1)S(1)}, u32[]{:S(2)}, u32[]{:S(2)}) %collective-permute-start.41) | collective-permute-done | bytes 262176 | tf_op jit(solution)/shard_map/ppermute | solution.py:350
  121.0 2.7 %shard_map.74.refs_4_ = f32[1024,2048]{1,0:T(8,128)S(1)} custom-call(s32[3]{0:T(128)S(1)} %pad_add_fusion.ids, bf16[1024,1024]{1,0:T(8,128)(2,1)S(1)} %shard_map.68.s, bf16[64,2048]{1,0:T(8,128)(2,1)S(1)} %collective-permute-done.33.refs_0_.refs_2_, bf16[64,2048]{1,0:T(8,128)(2,1)S(1)} %collective-permute-done.34.refs_1_.refs_3_, ...), custom_call_target="tpu_custom_call", output_to_operand_aliasing={{}: (6, {})} | custom-call | flops 1073741824 | bytes 8388608 | tf_op jit(solution)/shard_map/pallas_call | solution.py:269
  123.7 2.7 %shard_map.75.acc = f32[1024,2048]{1,0:T(8,128)S(1)} custom-call(s32[3]{0:T(128)S(1)} %pad_add_fusion.ids, bf16[1024,1024]{1,0:T(8,128)(2,1)S(1)} %shard_map.68.s, bf16[64,2048]{1,0:T(8,128)(2,1)S(1)} %collective-permute-done.20.refs_0_.refs_10_, bf16[64,2048]{1,0:T(8,128)(2,1)S(1)} %collective-permute-done.21.refs_1_.refs_11_, ...), custom_call_target="tpu_custom_call", output_to_operand_aliasing={{}: (6, {})} | custom-call | flops 1073741824 | bytes 8388608 | tf_op jit(solution)/shard_map/pallas_call | solution.py:269
  126.5 3.7 %last.1 = (bf16[1024,2048]{1,0:T(8,128)(2,1)}, bf16[128,1024]{1,0:T(8,128)(2,1)}) custom-call(s32[3]{0:T(128)S(1)} %pad_add_fusion.ids, bf16[1024,1024]{1,0:T(8,128)(2,1)S(1)} %shard_map.68.s, f32[1024,2048]{1,0:T(8,128)S(1)} %shard_map.75.acc, bf16[64,2048]{1,0:T(8,128)(2,1)S(1)} %pad_maximum_fusion.1.refs_0_, ...), custom_call_target="tpu_custom_call" | custom-call | flops 1073741824 | bytes 8388608 | tf_op jit(solution)/shard_map/last/pallas_call | solution.py:309
  (100 shorter events, 33.5 us)
Async XLA Ops:
  7.3 21.4 %collective-permute-start.27 = (bf16[64,2048]{1,0:T(8,128)(2,1)S(1)}, bf16[64,2048]{1,0:T(8,128)(2,1)S(1)}, u32[]{:S(2)}, u32[]{:S(2)}) collective-permute-start(bf16[64,2048]{1,0:T(8,128)(2,1)S(1)} %get-tuple-element.33), channel_id=1, source_target_pairs={{0,1},{1,0},{2,3},{3,2},{4,5},{5,4},{6,7},{7,6},{8,9},{9,8},{10,11... | collective-permute-start | bytes 786440 | tf_op jit(solution)/shard_map/ppermute | solution.py:350
  11.7 31.9 %collective-permute-start.24 = (bf16[64,2048]{1,0:T(8,128)(2,1)S(1)}, bf16[64,2048]{1,0:T(8,128)(2,1)S(1)}, u32[]{:S(2)}, u32[]{:S(2)}) collective-permute-start(bf16[64,2048]{1,0:T(8,128)(2,1)S(1)} %get-tuple-element.29), channel_id=1, source_target_pairs={{0,1},{1,0},{2,3},{3,2},{4,5},{5,4},{6,7},{7,6},{8,9},{9,8},{10,11... | collective-permute-start | bytes 786440 | tf_op jit(solution)/shard_map/ppermute | solution.py:350
  11.8 15.2 %collective-permute-start.9 = (bf16[128,2048]{1,0:T(8,128)(2,1)S(1)}, bf16[128,2048]{1,0:T(8,128)(2,1)S(1)}, u32[]{:S(2)}, u32[]{:S(2)}) collective-permute-start(bf16[128,2048]{1,0:T(8,128)(2,1)S(1)} %copy-done), channel_id=1, source_target_pairs={{0,4},{1,5},{2,6},{3,7},{4,0},{5,1},{6,2},{7,3},{8,12},{9,13},{10,... | collective-permute-start | bytes 1572872 | tf_op jit(solution)/shard_map/ppermute | solution.py:350
  15.8 27.9 %collective-permute-start.11 = (bf16[64,2048]{1,0:T(8,128)(2,1)S(1)}, bf16[64,2048]{1,0:T(8,128)(2,1)S(1)}, u32[]{:S(2)}, u32[]{:S(2)}) collective-permute-start(bf16[64,2048]{1,0:T(8,128)(2,1)S(1)} %upper.1), channel_id=1, source_target_pairs={{0,2},{1,3},{2,0},{3,1},{4,6},{5,7},{6,4},{7,5},{8,10},{9,11},{10,... | collective-permute-start | bytes 786440 | tf_op jit(solution)/shard_map/ppermute | solution.py:350
  27.0 18.3 %collective-permute-start.13 = (bf16[64,2048]{1,0:T(8,128)(2,1)S(1)}, bf16[64,2048]{1,0:T(8,128)(2,1)S(1)}, u32[]{:S(2)}, u32[]{:S(2)}) collective-permute-start(bf16[64,2048]{1,0:T(8,128)(2,1)S(1)} %slice.8), channel_id=1, source_target_pairs={{0,2},{1,3},{2,0},{3,1},{4,6},{5,7},{6,4},{7,5},{8,10},{9,11},{10,... | collective-permute-start | bytes 786440 | tf_op jit(solution)/shard_map/ppermute | solution.py:350
  30.0 11.8 %collective-permute-start.5 = (bf16[64,2048]{1,0:T(8,128)(2,1)S(1)}, bf16[64,2048]{1,0:T(8,128)(2,1)S(1)}, u32[]{:S(2)}, u32[]{:S(2)}) collective-permute-start(bf16[64,2048]{1,0:T(8,128)(2,1)S(1)} %add_convert_fusion.6), channel_id=1, source_target_pairs={{0,2},{1,3},{2,0},{3,1},{4,6},{5,7},{6,4},{7,5},{8,10},{9,11},{10,... | collective-permute-start | bytes 786440 | tf_op jit(solution)/shard_map/ppermute | solution.py:350
  31.7 14.7 %collective-permute-start.26 = (bf16[64,2048]{1,0:T(8,128)(2,1)S(1)}, bf16[64,2048]{1,0:T(8,128)(2,1)S(1)}, u32[]{:S(2)}, u32[]{:S(2)}) collective-permute-start(bf16[64,2048]{1,0:T(8,128)(2,1)S(1)} %add_convert_fusion.3), channel_id=1, source_target_pairs={{0,2},{1,3},{2,0},{3,1},{4,6},{5,7},{6,4},{7,5},{8,10},{9,11},{10,... | collective-permute-start | bytes 786440 | tf_op jit(solution)/shard_map/ppermute | solution.py:350
  43.7 13.4 %collective-permute-start.2 = (bf16[64,2048]{1,0:T(8,128)(2,1)S(1)}, bf16[64,2048]{1,0:T(8,128)(2,1)S(1)}, u32[]{:S(2)}, u32[]{:S(2)}) collective-permute-start(bf16[64,2048]{1,0:T(8,128)(2,1)S(1)} %add_convert_fusion.7), channel_id=1, source_target_pairs={{0,2},{1,3},{2,0},{3,1},{4,6},{5,7},{6,4},{7,5},{8,10},{9,11},{10,... | collective-permute-start | bytes 786440 | tf_op jit(solution)/shard_map/ppermute | solution.py:350
  48.9 10.5 %collective-permute-start.6 = (bf16[64,2048]{1,0:T(8,128)(2,1)S(1)}, bf16[64,2048]{1,0:T(8,128)(2,1)S(1)}, u32[]{:S(2)}, u32[]{:S(2)}) collective-permute-start(bf16[64,2048]{1,0:T(8,128)(2,1)S(1)} %add_convert_fusion.5), channel_id=1, source_target_pairs={{0,4},{1,5},{2,6},{3,7},{4,0},{5,1},{6,2},{7,3},{8,12},{9,13},{10,... | collective-permute-start | bytes 786440 | tf_op jit(solution)/shard_map/ppermute | solution.py:350
  51.5 28.7 %collective-permute-start.8 = (bf16[128,2048]{1,0:T(8,128)(2,1)S(1)}, bf16[128,2048]{1,0:T(8,128)(2,1)S(1)}, u32[]{:S(2)}, u32[]{:S(2)}) collective-permute-start(bf16[128,2048]{1,0:T(8,128)(2,1)S(1)} %copy-done.1), channel_id=1, source_target_pairs={{0,1},{1,0},{2,3},{3,2},{4,5},{5,4},{6,7},{7,6},{8,9},{9,8},{10,11... | collective-permute-start | bytes 1572872 | tf_op jit(solution)/shard_map/ppermute | solution.py:350
  54.5 9.6 %collective-permute-start.17 = (bf16[64,2048]{1,0:T(8,128)(2,1)S(1)}, bf16[64,2048]{1,0:T(8,128)(2,1)S(1)}, u32[]{:S(2)}, u32[]{:S(2)}) collective-permute-start(bf16[64,2048]{1,0:T(8,128)(2,1)S(1)} %slice.9), channel_id=1, source_target_pairs={{0,2},{1,3},{2,0},{3,1},{4,6},{5,7},{6,4},{7,5},{8,10},{9,11},{10,... | collective-permute-start | bytes 786440 | tf_op jit(solution)/shard_map/ppermute | solution.py:350
  57.1 24.4 %collective-permute-start.10 = (bf16[128,2048]{1,0:T(8,128)(2,1)S(1)}, bf16[128,2048]{1,0:T(8,128)(2,1)S(1)}, u32[]{:S(2)}, u32[]{:S(2)}) collective-permute-start(bf16[128,2048]{1,0:T(8,128)(2,1)S(1)} %collective-permute-done.9.refs_2_), channel_id=1, source_target_pairs={{0,1},{1,0},{2,3},{3,2},{4,5},{5,4},{6,7},{7,6},{8,9},{9,8},{10,11... | collective-permute-start | bytes 1572872 | tf_op jit(solution)/shard_map/ppermute | solution.py:350
  59.4 20.6 %collective-permute-start.31 = (bf16[64,2048]{1,0:T(8,128)(2,1)S(1)}, bf16[64,2048]{1,0:T(8,128)(2,1)S(1)}, u32[]{:S(2)}, u32[]{:S(2)}) collective-permute-start(bf16[64,2048]{1,0:T(8,128)(2,1)S(1)} %fusion.1), channel_id=1, source_target_pairs={{0,8},{1,9},{2,10},{3,11},{4,12},{5,13},{6,14},{7,15},{8,0},{9,1},... | collective-permute-start | bytes 786440 | tf_op jit(solution)/shard_map/ppermute | solution.py:350
  62.3 17.9 %collective-permute-start.16 = (bf16[64,2048]{1,0:T(8,128)(2,1)S(1)}, bf16[64,2048]{1,0:T(8,128)(2,1)S(1)}, u32[]{:S(2)}, u32[]{:S(2)}) collective-permute-start(bf16[64,2048]{1,0:T(8,128)(2,1)S(1)} %collective-permute-done.15.refs_8_), channel_id=1, source_target_pairs={{0,1},{1,0},{2,3},{3,2},{4,5},{5,4},{6,7},{7,6},{8,9},{9,8},{10,11... | collective-permute-start | bytes 786440 | tf_op jit(solution)/shard_map/ppermute | solution.py:350
  64.1 21.0 %collective-permute-start.7 = (bf16[64,2048]{1,0:T(8,128)(2,1)S(1)}, bf16[64,2048]{1,0:T(8,128)(2,1)S(1)}, u32[]{:S(2)}, u32[]{:S(2)}) collective-permute-start(bf16[64,2048]{1,0:T(8,128)(2,1)S(1)} %fusion), channel_id=1, source_target_pairs={{0,8},{1,9},{2,10},{3,11},{4,12},{5,13},{6,14},{7,15},{8,0},{9,1},... | collective-permute-start | bytes 786440 | tf_op jit(solution)/shard_map/ppermute | solution.py:350
  84.3 12.7 %collective-permute-start.32 = (bf16[64,1024]{1,0:T(8,128)(2,1)S(1)}, bf16[64,1024]{1,0:T(8,128)(2,1)S(1)}, u32[]{:S(2)}, u32[]{:S(2)}) collective-permute-start(bf16[64,1024]{1,0:T(8,128)(2,1)S(1)} %shard_map.72), channel_id=1, source_target_pairs={{0,8},{1,9},{2,10},{3,11},{4,12},{5,13},{6,14},{7,15},{8,0},{9,1},... | collective-permute-start | bytes 393224 | tf_op jit(solution)/shard_map/ppermute | solution.py:350
  87.1 12.1 %collective-permute-start.19 = (bf16[64,1024]{1,0:T(8,128)(2,1)S(1)}, bf16[64,1024]{1,0:T(8,128)(2,1)S(1)}, u32[]{:S(2)}, u32[]{:S(2)}) collective-permute-start(bf16[64,1024]{1,0:T(8,128)(2,1)S(1)} %shard_map.71), channel_id=1, source_target_pairs={{0,8},{1,9},{2,10},{3,11},{4,12},{5,13},{6,14},{7,15},{8,0},{9,1},... | collective-permute-start | bytes 393224 | tf_op jit(solution)/shard_map/ppermute | solution.py:350
  99.2 12.7 %collective-permute-start.20 = (bf16[64,2048]{1,0:T(8,128)(2,1)S(1)}, bf16[64,2048]{1,0:T(8,128)(2,1)S(1)}, u32[]{:S(2)}, u32[]{:S(2)}) collective-permute-start(bf16[64,2048]{1,0:T(8,128)(2,1)S(1)} %pad_maximum_fusion.refs_2_.refs_8_), channel_id=1, source_target_pairs={{0,2},{1,3},{2,0},{3,1},{4,6},{5,7},{6,4},{7,5},{8,10},{9,11},{10,... | collective-permute-start | bytes 786440 | tf_op jit(solution)/shard_map/ppermute | solution.py:350
  99.5 12.4 %collective-permute-start.38 = (bf16[64,2048]{1,0:T(8,128)(2,1)S(1)}, bf16[64,2048]{1,0:T(8,128)(2,1)S(1)}, u32[]{:S(2)}, u32[]{:S(2)}) collective-permute-start(bf16[64,2048]{1,0:T(8,128)(2,1)S(1)} %pad_maximum_fusion.refs_2_.refs_8_), channel_id=1, source_target_pairs={{0,1},{1,0},{2,3},{3,2},{4,5},{5,4},{6,7},{7,6},{8,9},{9,8},{10,11... | collective-permute-start | bytes 786440 | tf_op jit(solution)/shard_map/ppermute | solution.py:350
  99.5 12.4 %collective-permute-start.22 = (bf16[64,2048]{1,0:T(8,128)(2,1)S(1)}, bf16[64,2048]{1,0:T(8,128)(2,1)S(1)}, u32[]{:S(2)}, u32[]{:S(2)}) collective-permute-start(bf16[64,2048]{1,0:T(8,128)(2,1)S(1)} %pad_maximum_fusion.refs_2_.refs_8_), channel_id=1, source_target_pairs={{0,4},{1,5},{2,6},{3,7},{4,0},{5,1},{6,2},{7,3},{8,12},{9,13},{10,... | collective-permute-start | bytes 786440 | tf_op jit(solution)/shard_map/ppermute | solution.py:350
  106.8 10.2 %collective-permute-start.39 = (bf16[64,2048]{1,0:T(8,128)(2,1)S(1)}, bf16[64,2048]{1,0:T(8,128)(2,1)S(1)}, u32[]{:S(2)}, u32[]{:S(2)}) collective-permute-start(bf16[64,2048]{1,0:T(8,128)(2,1)S(1)} %collective-permute-done.35.refs_2_.refs_4_), channel_id=1, source_target_pairs={{0,2},{1,3},{2,0},{3,1},{4,6},{5,7},{6,4},{7,5},{8,10},{9,11},{10,... | collective-permute-start | bytes 786440 | tf_op jit(solution)/shard_map/ppermute | solution.py:350
  111.9 11.8 %collective-permute-start.21 = (bf16[64,2048]{1,0:T(8,128)(2,1)S(1)}, bf16[64,2048]{1,0:T(8,128)(2,1)S(1)}, u32[]{:S(2)}, u32[]{:S(2)}) collective-permute-start(bf16[64,2048]{1,0:T(8,128)(2,1)S(1)} %collective-permute-done.20.refs_0_.refs_10_), channel_id=1, source_target_pairs={{0,1},{1,0},{2,3},{3,2},{4,5},{5,4},{6,7},{7,6},{8,9},{9,8},{10,11... | collective-permute-start | bytes 786440 | tf_op jit(solution)/shard_map/ppermute | solution.py:350
  112.4 11.3 %collective-permute-start.23 = (bf16[64,2048]{1,0:T(8,128)(2,1)S(1)}, bf16[64,2048]{1,0:T(8,128)(2,1)S(1)}, u32[]{:S(2)}, u32[]{:S(2)}) collective-permute-start(bf16[64,2048]{1,0:T(8,128)(2,1)S(1)} %collective-permute-done.22.refs_2_.refs_12_), channel_id=1, source_target_pairs={{0,1},{1,0},{2,3},{3,2},{4,5},{5,4},{6,7},{7,6},{8,9},{9,8},{10,11... | collective-permute-start | bytes 786440 | tf_op jit(solution)/shard_map/ppermute | solution.py:350
  117.0 9.5 %collective-permute-start.40 = (bf16[64,2048]{1,0:T(8,128)(2,1)S(1)}, bf16[64,2048]{1,0:T(8,128)(2,1)S(1)}, u32[]{:S(2)}, u32[]{:S(2)}) collective-permute-start(bf16[64,2048]{1,0:T(8,128)(2,1)S(1)} %collective-permute-done.39.refs_6_), channel_id=1, source_target_pairs={{0,1},{1,0},{2,3},{3,2},{4,5},{5,4},{6,7},{7,6},{8,9},{9,8},{10,11... | collective-permute-start | bytes 786440 | tf_op jit(solution)/shard_map/ppermute | solution.py:350
  (25 other events, 185.1 us)
